TPU v7x, 256 devices: a whole 4x4x8 slice. The times are simulated.
256 devices in a mesh: seq: 32 (over z, y), head: 8 (over x, core).
Axes of the slice: x: 4, y: 4, z: 8, core: 2. Of those that a mesh axis runs over, the one named last changes fastest.
Arguments:
- x_in: bfloat16 [4096, 8192], P('seq', 'head'), may hold values from -6 to 6
- z_gate: bfloat16 [4096, 8192], P('seq', 'head'), may hold values from -6 to 6
- b_in: bfloat16 [4096, 2048], P('seq', 'head'), may hold values from -0.75 to 0.75
- c_in: bfloat16 [4096, 2048], P('seq', 'head'), may hold values from -0.75 to 0.75
- log_decay: float32 [4096, 128], P('seq', 'head'), may hold values from 0 to 1.5
- step_size: float32 [4096, 128], P('seq', 'head'), may hold values from 0.3 to 3
- d_skip: float32 [128], P('head'), may hold values from 0.5 to 2
- norm_gain: float32 [8192], P('head'), may hold values from 0.25 to 1.75
- w_out: bfloat16 [8192, 4096], P('head'), may hold values from -0.0625 to 0.0625
- residual: bfloat16 [4096, 4096], P(('seq', 'head')), may hold values from -8 to 8
- final_gain: float32 [4096], replicated, may hold values from 0.25 to 1.75
- vocab: bfloat16 [65536, 4096], P(('seq', 'head')), may hold values from -12 to 12
- targets: int32 [32, 128], P(None, 'head'), may hold values from 0 to 65535
Outputs:
- hidden_out: float32 [4096, 4096], P(('seq', 'head'))
- logprob: float32 [4096], P(('seq', 'head'))
All inputs are finite; a program needn't handle non-finite values.
Results may differ from a plain program's by a relative error of at most 0.0029.
Values may be sent and summed in bfloat16 or wider, within the bound.
No kernel may reach another device: no remote copies, remote signals or barrier semaphores. Data moves between devices by JAX's collectives and lax.ppermute only.
A program may use at most 128 MiB of HBM per device.

v0:
```python
import jax
import jax.numpy as jnp
from jax import lax
from jax.sharding import PartitionSpec as P

SCAN_LANE_NUMBER = 128
HEAD_DIM = 64
STATE = 256
GROUPS = 8
INNER = 8192
epsilon = 1e-05
highest = lax.Precision.HIGHEST


def carried_in(value, axis, combine, identity):
    count, mine = (lax.axis_size(axis), lax.axis_index(axis))
    everything = jax.tree.map(lambda part: lax.all_gather(part, axis), value)
    start = jax.tree.map(
        lambda part, zero: jnp.broadcast_to(jnp.asarray(zero, part.dtype), part.shape),
        value,
        identity,
    )

    def hop(k, before):
        reached = k < mine
        new = combine(before, jax.tree.map(lambda part: part[k], everything))
        return jax.tree.map(lambda a, b: jnp.where(reached, a, b), new, before)

    return lax.fori_loop(0, count, hop, start)


def joined(part, axis, combine):
    gathered = jax.tree.map(lambda a: lax.all_gather(a, axis), part)

    def take(source):
        return jax.tree.map(lambda a: lax.dynamic_index_in_dim(a, source, 0, False), gathered)

    return lax.fori_loop(
        1, lax.axis_size(axis), lambda source, state: combine(state, take(source)), take(0)
    )


def local_terms(inputs, b_rows, c_rows, decays, step_rows, per_group):
    length = inputs.shape[0]
    cumulative = jnp.cumsum(decays, axis=0)
    by_head = cumulative.T
    gaps = by_head[:, None, :] - by_head[:, :, None]
    positions = jnp.arange(length)
    causal = positions[None, :] <= positions[:, None]
    segment_w = jnp.where(causal[None], jnp.exp(jnp.minimum(gaps, 0.0)), 0.0)
    scores = jnp.einsum("tgn,sgn->gts", c_rows, b_rows, precision=highest)
    head_scores = jnp.repeat(scores, per_group, axis=0)
    weights = segment_w * head_scores * step_rows.T[:, None, :]
    within = jnp.einsum("hts,shp->thp", weights, inputs, precision=highest)
    last = cumulative[-1]
    end_weight = jnp.exp(last[None, :] - cumulative) * step_rows
    b_heads = jnp.repeat(b_rows, per_group, axis=1)
    end_state = jnp.einsum(
        "shp,shn->hpn", inputs * end_weight[:, :, None], b_heads, precision=highest
    )
    return (within, cumulative, end_state, jnp.exp(-last))


def carried(c_rows, cumulative, state, per_group):
    c_heads = jnp.repeat(c_rows, per_group, axis=1)
    return jnp.exp(-cumulative)[:, :, None] * jnp.einsum(
        "thn,hpn->thp", c_heads, state, precision=highest
    )


def chain(earlier, later):
    return (earlier[0] * later[0], later[0][:, None, None] * earlier[1] + later[1])


def vocab_fold(token_all, wanted, offset):

    def update(carry, piece, start):
        top, total, picked = carry
        logits = lax.dot_general(
            token_all, piece, (((1,), (1,)), ((), ())), preferred_element_type=jnp.float32
        )
        new_top = jnp.max(logits, axis=1)
        total = total * jnp.exp(top - new_top) + jnp.sum(jnp.exp(logits - new_top[:, None]), axis=1)
        vocab_ids = offset + lax.broadcasted_iota(jnp.int32, (1, piece.shape[0]), 1)
        picked = jnp.sum(jnp.where(vocab_ids == wanted[:, None], logits, 0.0), axis=1)
        return (new_top, total, picked)

    return update


def combine(first, second):
    top = jnp.maximum(first[0], second[0])
    total = first[1] * jnp.exp(first[0] - top) + second[1] * jnp.exp(second[0] - top)
    return (top, total, first[2] + second[2])


def start_triple(count):
    return (
        jnp.full((count,), -jnp.inf, jnp.float32),
        jnp.zeros((count,), jnp.float32),
        jnp.zeros((count,), jnp.float32),
    )


def shards(
    x_in,
    z_gate,
    b_in,
    c_in,
    log_decay,
    step_size,
    d_skip,
    norm_gain,
    w_out,
    residual,
    final_gain,
    vocab,
    targets,
):
    per_group = SCAN_LANE_NUMBER // GROUPS
    length = x_in.shape[0]
    head_count = log_decay.shape[1]
    group_count = b_in.shape[1] // STATE
    inputs = x_in.astype(jnp.float32).reshape(length, head_count, HEAD_DIM)
    b_rows = b_in.astype(jnp.float32).reshape(length, group_count, STATE)
    c_rows = c_in.astype(jnp.float32).reshape(length, group_count, STATE)
    within, cumulative, end_state, decay = local_terms(
        inputs, b_rows, c_rows, log_decay, step_size, per_group
    )
    identity = (jnp.ones_like(decay), jnp.zeros_like(end_state))
    incoming = carried_in((decay, end_state), "seq", chain, identity)
    mixed = (
        within
        + carried(c_rows, cumulative, incoming[1], per_group)
        + d_skip[None, :, None] * inputs
    )
    gated = mixed.reshape(length, head_count * HEAD_DIM) * jax.nn.silu(z_gate.astype(jnp.float32))
    grouped = gated.reshape(length, group_count, INNER // GROUPS)
    scaled = grouped * lax.rsqrt(jnp.mean(grouped * grouped, axis=-1, keepdims=True) + epsilon)
    normed_inner = (scaled.reshape(length, head_count * HEAD_DIM) * norm_gain).astype(jnp.bfloat16)
    rows = length // lax.axis_size("head")
    summed = lax.psum_scatter(
        jnp.dot(normed_inner, w_out, preferred_element_type=jnp.float32),
        "head",
        scatter_dimension=0,
        tiled=True,
    )
    hidden_out = residual.astype(jnp.float32) + summed
    normed = (
        hidden_out
        * lax.rsqrt(jnp.mean(hidden_out * hidden_out, axis=-1, keepdims=True) + epsilon)
        * final_gain
    ).astype(jnp.bfloat16)
    token_all = lax.all_gather(normed, "seq", axis=0, tiled=True)
    wanted = targets.reshape(-1)
    offset = lax.axis_index("seq") * (vocab.shape[0] * lax.axis_size("head"))
    update = vocab_fold(token_all, wanted, offset)
    top, total, picked = update(
        start_triple(token_all.shape[0]),
        lax.all_gather(vocab, "head", axis=0, tiled=True),
        jnp.int32(0),
    )
    top, total, picked = joined((top, total, picked), "seq", combine)
    every = picked - top - jnp.log(total)
    logprob = lax.dynamic_slice_in_dim(every, lax.axis_index("seq") * rows, rows, 0)
    return (hidden_out, logprob)


def solution(mesh):
    return jax.shard_map(
        shards,
        mesh=mesh,
        in_specs=(
            P("seq", "head"),
            P("seq", "head"),
            P("seq", "head"),
            P("seq", "head"),
            P("seq", "head"),
            P("seq", "head"),
            P("head"),
            P("head"),
            P("head", None),
            P(("seq", "head"), None),
            P(),
            P(("seq", "head"), None),
            P(None, "head"),
        ),
        out_specs=(P(("seq", "head"), None), P(("seq", "head"))),
        check_vma=False,
    )
```

profile of v0, /device:TPU:2, one launch (start us, length us, event | category | flops | bytes accessed | tf_op | source)
XLA Modules:
  0.0 679.8 jit_solution(15846469999163818144)
XLA Ops:
  11.1 2.0 fusion.5
  14.2 43.4 %all-gather.3 = f32[32,1,16]{2,1,0:T(1,128)S(1)} all-gather(f32[1,1,16]{2,1,0:T(1,128)S(1)} %get-tuple-element.331), channel_id=1, replica_groups=mesh['seq'=32,'head'=8] {'seq'}, dimensions={0}, use_global_device_ids=true | all-gather | bytes 2112 | tf_op jit(solution)/shard_map/all_gather | solution.py:17
  59.2 190.0 %all-gather.15.cloned.1.call-done = f32[512,64,256]{2,1,0:T(8,128)} async-done(((f32[16,64,256]{2,1,0:T(8,128)}), f32[512,64,256]{2,1,0:T(8,128)}) %all-gather.15.cloned.1.call-update) | async-done | bytes 33554448 | tf_op jit(solution)/shard_map/all_gather | solution.py:17
  249.2 48.2 %while.34 = (s32[]{:T(128)}, f32[16,64,256]{2,1,0:T(8,128)S(1)}, s32[]{:T(128)}, f32[32,16]{1,0:T(8,128)S(1)}, f32[32,16,64,256]{3,2,1,0:T(8,128)}, /*index=5*/s32[]{:T(128)}, s32[]{:T(128)}) while((s32[]{:T(128)}, f32[16,64,256]{2,1,0:T(8,128)S(1)}, s32[]{:T(128)}, f32[32,16]{1,0:T(8,128)S(1)}, f32[32,16,64,256]{3,2,1,0:T(8,128)}, ...), condition=%wide.region_2.3_spmd.clone, body=%wide.region_1.2_spmd.clone.sunk | while | flops 1048580 | bytes 3146025 | solution.py:29
  249.2 1.5 fusion.39
  250.7 1.5 fusion.39
  252.2 1.5 fusion.39
  253.7 1.5 fusion.39
  255.2 1.5 fusion.39
  256.7 1.5 fusion.39
  258.3 1.5 fusion.39
  259.8 1.5 fusion.39
  261.3 1.5 fusion.39
  262.8 1.5 fusion.39
  264.3 1.5 fusion.39
  265.8 1.5 fusion.39
  267.3 1.5 fusion.39
  268.8 1.5 fusion.39
  271.8 1.5 fusion.39
  280.8 1.5 fusion.39
  282.3 1.5 fusion.39
  291.4 1.5 fusion.39
  297.4 2.3 fusion.3
  300.1 6.1 fusion.23
  307.1 29.6 %reduce-scatter.2.cloned.1.call-done = f32[16,4096]{1,0:T(8,128)} async-done(((f32[128,4096]{1,0:T(8,128)}), f32[16,4096]{1,0:T(8,128)}) %reduce-scatter.2.cloned.1.call-update) | async-done | bytes 262160 | tf_op jit(solution)/shard_map/reduce_scatter | solution.py:142
  338.7 89.0 %all-gather.13.cloned.1.call-done = bf16[2048,4096]{1,0:T(8,128)(2,1)} async-done(((bf16[256,4096]{1,0:T(8,128)(2,1)}), bf16[2048,4096]{1,0:T(8,128)(2,1)}) %all-gather.13.cloned.1.call-update) | async-done | bytes 16777232 | tf_op jit(solution)/shard_map/all_gather | solution.py:160
  427.8 85.3 %all-gather.11.cloned.1.call-done = bf16[512,4096]{1,0:T(8,128)(2,1)} async-done(((bf16[16,4096]{1,0:T(8,128)(2,1)}), bf16[512,4096]{1,0:T(8,128)(2,1)}) %all-gather.11.cloned.1.call-update) | async-done | bytes 4194320 | tf_op jit(solution)/shard_map/all_gather | solution.py:154
  513.0 13.3 %fusion.29 = (f32[512]{0:T(512)S(1)}, f32[512,2048]{1,0:T(8,128)S(1)}) fusion(bf16[512,4096]{1,0:T(8,128)(2,1)} %all-gather.11.cloned.1.call-done, bf16[2048,4096]{1,0:T(8,128)(2,1)} %all-gather.13.cloned.1.call-done), kind=kOutput, calls=%fused_computation.60 | convolution fusion | flops 8590983168 | bytes 25167872 | tf_op jit(solution)/shard_map/dot_general | solution.py:79
  527.5 47.6 %all-gather.5 = f32[32,1,512]{2,1,0:T(1,128)S(1)} all-gather(f32[1,1,512]{2,1,0:T(1,128)S(1)} %bitcast.80), channel_id=1, replica_groups=mesh['seq'=32,'head'=8] {'seq'}, dimensions={0}, use_global_device_ids=true | all-gather | bytes 67584 | tf_op jit(solution)/shard_map/all_gather | solution.py:33
  575.1 47.0 %all-gather.6 = f32[32,1,512]{2,1,0:T(1,128)S(1)} all-gather(f32[1,1,512]{2,1,0:T(1,128)S(1)} %bitcast.78), channel_id=4, replica_groups=mesh['seq'=32,'head'=8] {'seq'}, dimensions={0}, use_global_device_ids=true | all-gather | bytes 67584 | tf_op jit(solution)/shard_map/all_gather | solution.py:33
  622.1 47.6 %all-gather.4 = f32[32,1,512]{2,1,0:T(1,128)S(1)} all-gather(f32[1,1,512]{2,1,0:T(1,128)S(1)} %bitcast.76), channel_id=3, replica_groups=mesh['seq'=32,'head'=8] {'seq'}, dimensions={0}, use_global_device_ids=true | all-gather | bytes 67584 | tf_op jit(solution)/shard_map/all_gather | solution.py:33
  669.7 2.9 while.33
  (232 shorter events, 34.1 us)
Async XLA Ops:
  7.2 50.6 %copy-start.6 = (f32[128,16]{0,1:T(8,128)S(1)}, f32[128,16]{0,1:T(8,128)}, u32[]{:S(2)}) copy-start(f32[128,16]{0,1:T(8,128)} %param.22) | copy-start | bytes 24580
  7.2 50.4 %copy-start.1 = (bf16[128,256]{1,0:T(8,128)(2,1)S(1)}, bf16[128,256]{1,0:T(8,128)(2,1)}, u32[]{:S(2)}) copy-start(bf16[128,256]{1,0:T(8,128)(2,1)} %param.19) | copy-start | bytes 196612
  7.2 50.4 %copy-start.2 = (bf16[128,256]{1,0:T(8,128)(2,1)S(1)}, bf16[128,256]{1,0:T(8,128)(2,1)}, u32[]{:S(2)}) copy-start(bf16[128,256]{1,0:T(8,128)(2,1)} %param.20) | copy-start | bytes 196612
  7.2 242.0 %all-gather.15.cloned.1.call-start = ((), (), s32[]{:S(2)}) async-start(), calls=%async_computation.4 | async-start | bytes 34603008 | tf_op jit(solution)/shard_map/all_gather | solution.py:17
  13.1 323.5 %reduce-scatter.2.cloned.1.call-start = ((), (), s32[]{:S(2)}) async-start(), calls=%async_computation.1 | async-start | bytes 2359296 | tf_op jit(solution)/shard_map/reduce_scatter | solution.py:142
  249.2 48.2 %copy-start.8 = (f32[16]{0:T(128)S(1)}, f32[16]{0:T(128)}, u32[]{:S(2)}) copy-start(f32[16]{0:T(128)} %param.23) | copy-start | bytes 196
  249.2 50.7 %copy-start.3 = (bf16[128,1024]{1,0:T(8,128)(2,1)S(1)}, bf16[128,1024]{1,0:T(8,128)(2,1)}, u32[]{:S(2)}) copy-start(bf16[128,1024]{1,0:T(8,128)(2,1)} %param.18) | copy-start | bytes 786436
  297.3 2.8 copy-start.9
  306.3 30.4 %copy-start.4 = (bf16[16,4096]{1,0:T(8,128)(2,1)S(1)}, bf16[16,4096]{1,0:T(8,128)(2,1)}, u32[]{:S(2)}) copy-start(bf16[16,4096]{1,0:T(8,128)(2,1)} %param.26) | copy-start | bytes 393220
  306.3 31.5 %copy-start.5 = (f32[4096]{0:T(1024)S(1)}, f32[4096]{0:T(1024)}, u32[]{:S(2)}) copy-start(f32[4096]{0:T(1024)} %param.27) | copy-start | bytes 49156
  306.3 32.3 %copy-start.7 = (s32[32,16]{0,1:T(8,128)S(1)}, s32[32,16]{0,1:T(8,128)}, u32[]{:S(2)}) copy-start(s32[32,16]{0,1:T(8,128)} %param.29) | copy-start | bytes 6148
  306.3 121.5 %all-gather.13.cloned.1.call-start = ((), (), s32[]{:S(2)}) async-start(), calls=%async_computation.3 | async-start | bytes 18874368 | tf_op jit(solution)/shard_map/all_gather | solution.py:160
  307.0 206.0 %all-gather.11.cloned.1.call-start = ((), (), s32[]{:S(2)}) async-start(), calls=%async_computation.2 | async-start | bytes 4325376 | tf_op jit(solution)/shard_map/all_gather | solution.py:154
  337.8 188.5 %copy-start = (f32[16,4096]{1,0:T(8,128)}, f32[16,4096]{1,0:T(8,128)S(1)}, u32[]{:S(2)}) copy-start(f32[16,4096]{1,0:T(8,128)S(1)} %get-tuple-element.325) | copy-start | bytes 786436
Sparse Core Ops, SparseCore 0:
  13.2 235.8 all-gather.14
  306.4 30.1 reduce-scatter.1
  338.5 89.1 all-gather.12
  430.2 82.7 all-gather.10
where the time goes:
time: 681 us; the launch traced here: 680 us
  waiting for transfers between devices  395 us (58%)
  blocking collectives  186 us (27%)
  other arithmetic  53.1 us (8%)
  matrix products  25.1 us (4%)
  between operations  14 us (2%)
    all_gather x1, waiting for transfers between devices, carried_in(): everything = jax.tree.map(lambda part: lax.all_gather(part, axis), value)  190 us
    all_gather x3, blocking collectives, joined(): gathered = jax.tree.map(lambda a: lax.all_gather(a, axis), part)  142 us
    all_gather x1, waiting for transfers between devices, shards(): lax.all_gather(vocab, 'head', axis=0, tiled=True)  89 us
    all_gather x1, waiting for transfers between devices, shards(): token_all = lax.all_gather(normed, 'seq', axis=0, tiled=True)  85.3 us
    select_n x32, other arithmetic, hop(): return jax.tree.map(lambda a, b: jnp.where(reached, a, b), new, before)  46.9 us
    all_gather x1, blocking collectives, carried_in(): everything = jax.tree.map(lambda part: lax.all_gather(part, axis), value)  43.4 us
    reduce_scatter x1, waiting for transfers between devices, shards(): lax.psum_scatter(jnp.dot(normed_inner, w_out, preferred_element_type=jnp....  29.6 us
  transfers between devices with their start and end apart: 4, of which 4 were waited for; matrix products, arithmetic and copies ran while one was open for 1% of the time, Pallas kernels for 0%

commit v1 on v0

--- a/solution.py
+++ b/solution.py
@@ -151,7 +151,9 @@
         * lax.rsqrt(jnp.mean(hidden_out * hidden_out, axis=-1, keepdims=True) + epsilon)
         * final_gain
     ).astype(jnp.bfloat16)
-    token_all = lax.all_gather(normed, "seq", axis=0, tiled=True)
+    token_all = jnp.concatenate(
+        lax.all_to_all(jnp.stack([normed] * lax.axis_size("seq")), "seq", 0, 0), axis=0
+    )
     wanted = targets.reshape(-1)
     offset = lax.axis_index("seq") * (vocab.shape[0] * lax.axis_size("head"))
     update = vocab_fold(token_all, wanted, offset)

time: 681 us -> 619 us (0.909)
  waiting for transfers between devices: 395 us -> 314 us
  starting transfers between devices: 0.16 us -> 10.2 us
    all_gather x1 -> x0, waiting for transfers between devices: 85.3 us -> none  [shards(): token_all = lax.all_gather(normed, 'seq', axis=0, tiled=True)]
    all_to_all x0 -> x1, waiting for transfers between devices: none -> 16.9 us  [shards(): lax.all_to_all(jnp.stack([normed] * lax.axis_size('seq')), 'seq', 0, 0)]
    all_gather x1, waiting for transfers between devices: 89 us -> 77 us  [shards(): lax.all_gather(vocab, 'head', axis=0, tiled=True)]
    all_to_all x0 -> x1, starting transfers between devices: none -> 10 us  [shards(): lax.all_to_all(jnp.stack([normed] * lax.axis_size('seq')), 'seq', 0, 0)]
where the time goes in v1:
time: 619 us; the launch traced here: 614 us
  waiting for transfers between devices  314 us (51%)
  blocking collectives  188 us (30%)
  other arithmetic  52.4 us (8%)
  matrix products  25.1 us (4%)
  between operations  14 us (2%)
  starting transfers between devices  10.2 us (2%)
  local copies, waits for them, and re-layouts  7.5 us (1%)
    all_gather x1, waiting for transfers between devices, carried_in(): everything = jax.tree.map(lambda part: lax.all_gather(part, axis), value)  190 us
    all_gather x3, blocking collectives, joined(): gathered = jax.tree.map(lambda a: lax.all_gather(a, axis), part)  144 us
    all_gather x1, waiting for transfers between devices, shards(): lax.all_gather(vocab, 'head', axis=0, tiled=True)  77 us
    select_n x32, other arithmetic, hop(): return jax.tree.map(lambda a, b: jnp.where(reached, a, b), new, before)  46.9 us
    all_gather x1, blocking collectives, carried_in(): everything = jax.tree.map(lambda part: lax.all_gather(part, axis), value)  43.4 us
    reduce_scatter x1, waiting for transfers between devices, shards(): lax.psum_scatter(jnp.dot(normed_inner, w_out, preferred_element_type=jnp....  29.7 us
    all_to_all x1, waiting for transfers between devices, shards(): lax.all_to_all(jnp.stack([normed] * lax.axis_size('seq')), 'seq', 0, 0)  16.9 us
    dot_general x1, matrix products, update(): lax.dot_general(token_all, piece, (((1,), (1,)), ((), ())), preferred_ele...  13.3 us
  transfers between devices with their start and end apart: 4, of which 4 were waited for; matrix products, arithmetic and copies ran while one was open for 1% of the time, Pallas kernels for 0%

profile of v1, /device:TPU:2, one launch (start us, length us, event | category | flops | bytes accessed | tf_op | source)
XLA Modules:
  0.0 613.6 jit_solution(16819321133181599598)
XLA Ops:
  11.1 2.0 fusion.5
  14.2 43.4 %all-gather.3 = f32[32,1,16]{2,1,0:T(1,128)S(1)} all-gather(f32[1,1,16]{2,1,0:T(1,128)S(1)} %get-tuple-element.331), channel_id=1, replica_groups=mesh['seq'=32,'head'=8] {'seq'}, dimensions={0}, use_global_device_ids=true | all-gather | bytes 2112 | tf_op jit(solution)/shard_map/all_gather | solution.py:17
  59.1 190.0 %all-gather.12.cloned.1.call-done = f32[512,64,256]{2,1,0:T(8,128)} async-done(((f32[16,64,256]{2,1,0:T(8,128)}), f32[512,64,256]{2,1,0:T(8,128)}) %all-gather.12.cloned.1.call-update) | async-done | bytes 33554448 | tf_op jit(solution)/shard_map/all_gather | solution.py:17
  249.2 48.2 %while.34 = (s32[]{:T(128)}, f32[16,64,256]{2,1,0:T(8,128)S(1)}, s32[]{:T(128)}, f32[32,16]{1,0:T(8,128)S(1)}, f32[32,16,64,256]{3,2,1,0:T(8,128)}, /*index=5*/s32[]{:T(128)}, s32[]{:T(128)}) while((s32[]{:T(128)}, f32[16,64,256]{2,1,0:T(8,128)S(1)}, s32[]{:T(128)}, f32[32,16]{1,0:T(8,128)S(1)}, f32[32,16,64,256]{3,2,1,0:T(8,128)}, ...), condition=%wide.region_2.3_spmd.clone, body=%wide.region_1.2_spmd.clone.sunk | while | flops 1048580 | bytes 3146025 | solution.py:29
  249.2 1.5 fusion.39
  250.7 1.5 fusion.39
  252.2 1.5 fusion.39
  253.7 1.5 fusion.39
  255.2 1.5 fusion.39
  256.7 1.5 fusion.39
  258.2 1.5 fusion.39
  259.7 1.5 fusion.39
  261.2 1.5 fusion.39
  262.8 1.5 fusion.39
  264.3 1.5 fusion.39
  265.8 1.5 fusion.39
  273.3 1.5 fusion.39
  282.3 1.5 fusion.39
  291.3 1.5 fusion.39
  292.8 1.5 fusion.39
  297.4 2.3 fusion.3
  300.1 6.1 fusion.23
  307.0 29.7 %reduce-scatter.2.cloned.1.call-done = f32[16,4096]{1,0:T(8,128)} async-done(((f32[128,4096]{1,0:T(8,128)}), f32[16,4096]{1,0:T(8,128)}) %reduce-scatter.2.cloned.1.call-update) | async-done | bytes 262160 | tf_op jit(solution)/shard_map/reduce_scatter | solution.py:142
  337.9 2.5 stack.2
  340.4 10.0 %all-to-all-start = ((bf16[32,16,4096]{2,1,0:T(8,128)(2,1)}), bf16[32,16,4096]{2,1,0:T(8,128)(2,1)}, u32[]{:S(2)}, u32[]{:S(2)}) async-start(bf16[32,16,4096]{2,1,0:T(8,128)(2,1)} %stack.2), calls=%async_computation.1 | async-start | bytes 8388608 | tf_op jit(solution)/shard_map/all_to_all | solution.py:155
  350.7 77.0 %all-gather.10.cloned.1.call-done = bf16[2048,4096]{1,0:T(8,128)(2,1)} async-done(((bf16[256,4096]{1,0:T(8,128)(2,1)}), bf16[2048,4096]{1,0:T(8,128)(2,1)}) %all-gather.10.cloned.1.call-update) | async-done | bytes 16777232 | tf_op jit(solution)/shard_map/all_gather | solution.py:162
  427.7 16.9 %all-to-all-done = bf16[32,16,4096]{2,1,0:T(8,128)(2,1)} async-done(((bf16[32,16,4096]{2,1,0:T(8,128)(2,1)}), bf16[32,16,4096]{2,1,0:T(8,128)(2,1)}, u32[]{:S(2)}, u32[]{:S(2)}) %all-to-all-start) | async-done | bytes 4194336 | tf_op jit(solution)/shard_map/all_to_all | solution.py:155
  444.6 13.3 %fusion.29 = (f32[512]{0:T(512)S(1)}, f32[512,2048]{1,0:T(8,128)S(1)}) fusion(bf16[512,4096]{1,0:T(8,128)(2,1)} %bitcast.13, bf16[2048,4096]{1,0:T(8,128)(2,1)} %all-gather.10.cloned.1.call-done), kind=kOutput, calls=%fused_computation.60 | convolution fusion | flops 8590983168 | bytes 25167872 | tf_op jit(solution)/shard_map/dot_general | solution.py:79
  459.0 49.9 %all-gather.5 = f32[32,1,512]{2,1,0:T(1,128)S(1)} all-gather(f32[1,1,512]{2,1,0:T(1,128)S(1)} %bitcast.81), channel_id=1, replica_groups=mesh['seq'=32,'head'=8] {'seq'}, dimensions={0}, use_global_device_ids=true | all-gather | bytes 67584 | tf_op jit(solution)/shard_map/all_gather | solution.py:33
  508.9 45.7 %all-gather.6 = f32[32,1,512]{2,1,0:T(1,128)S(1)} all-gather(f32[1,1,512]{2,1,0:T(1,128)S(1)} %bitcast.79), channel_id=4, replica_groups=mesh['seq'=32,'head'=8] {'seq'}, dimensions={0}, use_global_device_ids=true | all-gather | bytes 67584 | tf_op jit(solution)/shard_map/all_gather | solution.py:33
  554.7 48.9 %all-gather.4 = f32[32,1,512]{2,1,0:T(1,128)S(1)} all-gather(f32[1,1,512]{2,1,0:T(1,128)S(1)} %bitcast.77), channel_id=3, replica_groups=mesh['seq'=32,'head'=8] {'seq'}, dimensions={0}, use_global_device_ids=true | all-gather | bytes 67584 | tf_op jit(solution)/shard_map/all_gather | solution.py:33
  603.6 2.9 while.33
  (232 shorter events, 36.3 us)
Async XLA Ops:
  7.2 50.6 %copy-start.6 = (f32[128,16]{0,1:T(8,128)S(1)}, f32[128,16]{0,1:T(8,128)}, u32[]{:S(2)}) copy-start(f32[128,16]{0,1:T(8,128)} %param.22) | copy-start | bytes 24580
  7.2 50.4 %copy-start.1 = (bf16[128,256]{1,0:T(8,128)(2,1)S(1)}, bf16[128,256]{1,0:T(8,128)(2,1)}, u32[]{:S(2)}) copy-start(bf16[128,256]{1,0:T(8,128)(2,1)} %param.19) | copy-start | bytes 196612
  7.2 50.4 %copy-start.2 = (bf16[128,256]{1,0:T(8,128)(2,1)S(1)}, bf16[128,256]{1,0:T(8,128)(2,1)}, u32[]{:S(2)}) copy-start(bf16[128,256]{1,0:T(8,128)(2,1)} %param.20) | copy-start | bytes 196612
  7.2 241.9 %all-gather.12.cloned.1.call-start = ((), (), s32[]{:S(2)}) async-start(), calls=%async_computation.4 | async-start | bytes 34603008 | tf_op jit(solution)/shard_map/all_gather | solution.py:17
  13.1 323.6 %reduce-scatter.2.cloned.1.call-start = ((), (), s32[]{:S(2)}) async-start(), calls=%async_computation.2 | async-start | bytes 2359296 | tf_op jit(solution)/shard_map/reduce_scatter | solution.py:142
  249.1 48.2 %copy-start.8 = (f32[16]{0:T(128)S(1)}, f32[16]{0:T(128)}, u32[]{:S(2)}) copy-start(f32[16]{0:T(128)} %param.23) | copy-start | bytes 196
  249.2 50.7 %copy-start.3 = (bf16[128,1024]{1,0:T(8,128)(2,1)S(1)}, bf16[128,1024]{1,0:T(8,128)(2,1)}, u32[]{:S(2)}) copy-start(bf16[128,1024]{1,0:T(8,128)(2,1)} %param.18) | copy-start | bytes 786436
  297.3 2.8 copy-start.9
  306.2 30.5 %copy-start.4 = (bf16[16,4096]{1,0:T(8,128)(2,1)S(1)}, bf16[16,4096]{1,0:T(8,128)(2,1)}, u32[]{:S(2)}) copy-start(bf16[16,4096]{1,0:T(8,128)(2,1)} %param.26) | copy-start | bytes 393220
  306.2 31.6 %copy-start.5 = (f32[4096]{0:T(1024)S(1)}, f32[4096]{0:T(1024)}, u32[]{:S(2)}) copy-start(f32[4096]{0:T(1024)} %param.27) | copy-start | bytes 49156
  306.3 121.4 %all-gather.10.cloned.1.call-start = ((), (), s32[]{:S(2)}) async-start(), calls=%async_computation.3 | async-start | bytes 18874368 | tf_op jit(solution)/shard_map/all_gather | solution.py:162
  337.8 2.6 copy-start
  340.4 10.1 %copy-start.7 = (s32[32,16]{0,1:T(8,128)S(1)}, s32[32,16]{0,1:T(8,128)}, u32[]{:S(2)}) copy-start(s32[32,16]{0,1:T(8,128)} %param.29) | copy-start | bytes 6148
  340.4 104.1 %all-to-all-start = ((bf16[32,16,4096]{2,1,0:T(8,128)(2,1)}), bf16[32,16,4096]{2,1,0:T(8,128)(2,1)}, u32[]{:S(2)}, u32[]{:S(2)}) async-start(bf16[32,16,4096]{2,1,0:T(8,128)(2,1)} %stack.2), calls=%async_computation.1 | async-start | bytes 8388608 | tf_op jit(solution)/shard_map/all_to_all | solution.py:155
Sparse Core Ops, SparseCore 0:
  13.2 235.8 all-gather.11
  306.4 30.2 reduce-scatter.1
  338.6 89.0 all-gather.9
